TPU v7x, 32 devices: a whole 2x2x4 slice. The times are simulated.
32 devices in a mesh: img: 2 (over core), pix: 16 (over z, y, x).
Axes of the slice: x: 2, y: 2, z: 4, core: 2. Of those that a mesh axis runs over, the one named last changes fastest.
Arguments:
- latents: bfloat16 [2, 256, 1024], P('img'), may hold values from -6 to 6
- pixels: float32 [2, 3, 6144], P('img', None, 'pix'), may hold values from -5 to 5
- coords: int32 [2, 2, 6144], P('img', None, 'pix'), may hold values from 0 to 223, as said below
- kept_mask: int32 [2, 6144], P('img', 'pix'), may hold values from 0 to 1, as said below
- lat_gain: float32 [1024], replicated, may hold values from 0.1 to 1.9
- lat_shift: float32 [1024], replicated, may hold values from -3 to 3
- query_weight: bfloat16 [1024, 1024], replicated, may hold values from -0.1875 to 0.1875
- query_bias: float32 [1024], replicated, may hold values from -3 to 3
- in_gain: float32 [261], replicated, may hold values from 0.1 to 1.9
- in_shift: float32 [261], replicated, may hold values from -3 to 3
- key_weight: bfloat16 [261, 1024], replicated, may hold values from -0.75 to 0.75
- value_weight: bfloat16 [261, 1024], replicated, may hold values from -2.023352 to 2.023352
- value_bias: float32 [1024], replicated, may hold values from -4 to 4
- mlp_gain: float32 [1024], replicated, may hold values from 0.1 to 1.9
- mlp_shift: float32 [1024], replicated, may hold values from -3 to 3
- up_weight: bfloat16 [1024, 1024], replicated, may hold values from -0.1875 to 0.1875
- up_bias: float32 [1024], replicated, may hold values from -3 to 3
- down_weight: bfloat16 [1024, 1024], replicated, may hold values from -0.1875 to 0.1875
- down_bias: float32 [1024], replicated, may hold values from -3 to 3
- cotangent: bfloat16 [2, 256, 1024], P('img'), may hold values from -6 to 6
Outputs:
- encoded: bfloat16 [2, 256, 1024], P('img')
- latent_grad: float32 [2, 256, 1024], P('img')
- pixel_grad: float32 [2, 3, 6144], P('img', None, 'pix')
- lat_gain_grad: float32 [1024], replicated
- lat_shift_grad: float32 [1024], replicated
- query_weight_grad: float32 [1024, 1024], replicated
- query_bias_grad: float32 [1024], replicated
- in_gain_grad: float32 [261], replicated
- in_shift_grad: float32 [261], replicated
- key_weight_grad: float32 [261, 1024], replicated
- value_weight_grad: float32 [261, 1024], replicated
- value_bias_grad: float32 [1024], replicated
- mlp_gain_grad: float32 [1024], replicated
- mlp_shift_grad: float32 [1024], replicated
- up_weight_grad: float32 [1024, 1024], replicated
- up_bias_grad: float32 [1024], replicated
- down_weight_grad: float32 [1024, 1024], replicated
- down_bias_grad: float32 [1024], replicated
Inputs may be any that keep to these rules, and one draw needn't show every extreme that they name: `coords`: for each image the pixels are distinct cells of a 224 x 224 grid in row-major order, given as (row, column); the first and the last cell of the grid are always among them. `kept_mask`: exactly half of each image's pixels are kept; dropped keys cluster in square patches of 16 x 16 grid cells, with a share that varies by patch row.
All inputs are finite; a program needn't handle non-finite values.
Results may differ from a plain program's by a relative error of at most 0.017.
The roundings to bfloat16 on the way count: a program that leaves them out, or rounds other values in their place, can miss the bound.
Values may be sent and summed in bfloat16 or wider, within the bound.
No kernel may reach another device: no remote copies, remote signals or barrier semaphores. Data moves between devices by JAX's collectives and lax.ppermute only.
A program may use at most 128 MiB of HBM per device.

v0:
```python
from functools import partial
import math
import jax
import jax.numpy as jnp
from jax import lax
from jax.sharding import PartitionSpec as P

BANDS = 64
GRID = 224
EPSILON = 1e-05
HIGHEST = lax.Precision.HIGHEST
FLOOR = -1e30


def norm_axis(values, gain_vec, shift_vec, axis_pos):
    centre = values - jnp.mean(values, axis=axis_pos, keepdims=True)
    spread_sq = jnp.mean(centre * centre, axis=axis_pos, keepdims=True)
    return centre * lax.rsqrt(spread_sq + EPSILON) * gain_vec + shift_vec


def fourier_table(colors, grid_pos):
    position = grid_pos.astype(jnp.float32) * (2.0 / (GRID - 1)) - 1.0
    frequency = 1.0 + jnp.arange(BANDS, dtype=jnp.float32) * ((GRID / 2.0 - 1.0) / (BANDS - 1))
    phases = (position[:, None, :] * (math.pi * frequency)[None, :, None]).reshape(
        2 * BANDS, position.shape[1]
    )
    return jnp.concatenate([colors, position, jnp.sin(phases), jnp.cos(phases)], axis=0)


def contract(left, right, left_dim, right_dim, exact=None):
    return lax.dot_general(
        left,
        right,
        (((left_dim,), (right_dim,)), ((), ())),
        precision=exact,
        preferred_element_type=jnp.float32,
    )


def forward_pass(latents, pixels, coords, kept_mask, weights):
    (
        lat_gain,
        lat_shift,
        query_weight,
        query_bias,
        in_gain,
        in_shift,
        key_weight,
        value_weight,
        value_bias,
        mlp_gain,
        mlp_shift,
        up_weight,
        up_bias,
        down_weight,
        down_bias,
    ) = weights
    latent = latents[0].astype(jnp.float32)
    norm_one = norm_axis(latent, lat_gain, lat_shift, 1).astype(jnp.bfloat16)
    query = (
        jnp.dot(norm_one, query_weight, preferred_element_type=jnp.float32) + query_bias
    ).astype(jnp.bfloat16)
    table = fourier_table(pixels[0], coords[0]).astype(jnp.bfloat16)
    live_row = kept_mask[0].astype(jnp.bfloat16)
    slot_order = jnp.arange(live_row.shape[0], dtype=jnp.int32)
    table_full = table.astype(jnp.float32)
    x_in = norm_axis(table_full, in_gain[:, None], in_shift[:, None], 0).astype(jnp.bfloat16)
    keys = contract(x_in, key_weight, 0, 0).astype(jnp.bfloat16)
    values = (contract(x_in, value_weight, 0, 0) + value_bias).astype(jnp.bfloat16)
    inv_root = 1.0 / math.sqrt(query.shape[1])
    score = contract(query, keys, 1, 1) * inv_root
    live_mask = live_row > 0
    local_top = jnp.max(jnp.where(live_mask, score, FLOOR), axis=1)
    values_full = values.astype(jnp.float32)
    row_top = lax.pmax(local_top, "pix")
    weight = jnp.where(live_mask, jnp.exp(score - row_top[:, None]), 0.0)
    row_total, weighted = lax.psum(
        (jnp.sum(weight, axis=1), jnp.dot(weight, values_full, precision=HIGHEST)), "pix"
    )
    attn = weighted / row_total[:, None]
    mixed = latent + attn
    norm_two = norm_axis(mixed, mlp_gain, mlp_shift, 1).astype(jnp.bfloat16)
    pre_act = jnp.dot(norm_two, up_weight, preferred_element_type=jnp.float32) + up_bias
    hidden = jax.nn.gelu(pre_act, approximate=False).astype(jnp.bfloat16)
    encoded = mixed + jnp.dot(hidden, down_weight, preferred_element_type=jnp.float32) + down_bias
    saved = (
        latent,
        norm_one,
        query,
        table_full,
        x_in,
        keys,
        values,
        score,
        live_mask,
        row_top,
        row_total,
        attn,
        mixed,
        norm_two,
        pre_act,
        hidden,
        slot_order,
        slot_order,
    )
    return (encoded.astype(jnp.bfloat16)[None], saved)


def shards(
    latents,
    pixels,
    coords,
    kept_mask,
    lat_gain,
    lat_shift,
    query_weight,
    query_bias,
    in_gain,
    in_shift,
    key_weight,
    value_weight,
    value_bias,
    mlp_gain,
    mlp_shift,
    up_weight,
    up_bias,
    down_weight,
    down_bias,
    cotangent,
):
    weights = (
        lat_gain,
        lat_shift,
        query_weight,
        query_bias,
        in_gain,
        in_shift,
        key_weight,
        value_weight,
        value_bias,
        mlp_gain,
        mlp_shift,
        up_weight,
        up_bias,
        down_weight,
        down_bias,
    )
    encoded, saved = forward_pass(latents, pixels, coords, kept_mask, weights)
    fresh = lax.optimization_barrier((latents, pixels, coords, kept_mask, weights))
    discarded, saved = forward_pass(fresh[0], fresh[1], fresh[2], fresh[3], fresh[4])
    (
        latent,
        norm_one,
        query,
        table_full,
        x_in,
        keys,
        values,
        score,
        live_mask,
        row_top,
        row_total,
        attn,
        mixed,
        norm_two,
        pre_act,
        hidden,
        slot_order,
        kept_index,
    ) = saved
    inv_root = 1.0 / math.sqrt(query.shape[1])
    out_grad = cotangent[0]
    out_grad_full = out_grad.astype(jnp.float32)
    down_weight_grad = contract(hidden, out_grad, 0, 0)
    down_bias_grad = jnp.sum(out_grad_full, axis=0)
    hidden_grad = contract(out_grad, down_weight, 1, 1)
    ignored, gelu_pull = jax.vjp(partial(jax.nn.gelu, approximate=False), pre_act)
    pre_grad = gelu_pull(hidden_grad)[0].astype(jnp.bfloat16)
    up_weight_grad = contract(norm_two, pre_grad, 0, 0)
    up_bias_grad = jnp.sum(pre_grad.astype(jnp.float32), axis=0)
    norm_two_grad = contract(pre_grad, up_weight, 1, 1)
    ignored, mlp_pull = jax.vjp(partial(norm_axis, axis_pos=1), mixed, mlp_gain, mlp_shift)
    mixed_part, mlp_gain_grad, mlp_shift_grad = mlp_pull(norm_two_grad)
    mixed_grad = out_grad_full + mixed_part
    attn_grad = mixed_grad.astype(jnp.bfloat16)
    attn_grad_full = attn_grad.astype(jnp.float32)
    row_delta = jnp.sum(attn_grad_full * attn, axis=1)
    prob = jnp.where(live_mask, jnp.exp(score - row_top[:, None]), 0.0) / row_total[:, None]
    prob_grad = contract(attn_grad, values, 1, 1)
    score_grad = (prob * (prob_grad - row_delta[:, None])).astype(jnp.bfloat16)
    query_part = jnp.dot(score_grad, keys, preferred_element_type=jnp.float32) * inv_root
    key_grad = (contract(score_grad, query, 0, 0) * inv_root).astype(jnp.bfloat16)
    value_grad = contract(prob, attn_grad_full, 0, 0, HIGHEST).astype(jnp.bfloat16)
    key_weight_grad = contract(x_in, key_grad, 1, 0)
    value_weight_grad = contract(x_in, value_grad, 1, 0)
    value_bias_grad = jnp.sum(value_grad.astype(jnp.float32), axis=0)
    x_in_grad = contract(key_weight, key_grad, 1, 1) + contract(value_weight, value_grad, 1, 1)
    ignored, input_pull = jax.vjp(
        partial(norm_axis, axis_pos=0), table_full, in_gain[:, None], in_shift[:, None]
    )
    table_grad, in_gain_col, in_shift_col = input_pull(x_in_grad)
    color_grad = table_grad[:3]
    query_grad = lax.psum(query_part, "pix").astype(jnp.bfloat16)
    query_weight_grad = contract(norm_one, query_grad, 0, 0)
    query_bias_grad = jnp.sum(query_grad.astype(jnp.float32), axis=0)
    norm_one_grad = contract(query_grad, query_weight, 1, 1)
    ignored, latent_pull = jax.vjp(partial(norm_axis, axis_pos=1), latent, lat_gain, lat_shift)
    latent_part, lat_gain_grad, lat_shift_grad = latent_pull(norm_one_grad)
    latent_grad = mixed_grad + latent_part
    pixel_sums = lax.psum(
        (
            key_weight_grad,
            value_weight_grad,
            value_bias_grad,
            in_gain_col[:, 0],
            in_shift_col[:, 0],
        ),
        ("img", "pix"),
    )
    replica_sums = (
        lax.psum(lat_gain_grad.astype(jnp.bfloat16), "img").astype(jnp.float32),
        lax.psum(lat_shift_grad.astype(jnp.bfloat16), "img").astype(jnp.float32),
        lax.psum(query_weight_grad.astype(jnp.bfloat16), "img").astype(jnp.float32),
        lax.psum(query_bias_grad.astype(jnp.bfloat16), "img").astype(jnp.float32),
        lax.psum(mlp_gain_grad.astype(jnp.bfloat16), "img").astype(jnp.float32),
        lax.psum(mlp_shift_grad.astype(jnp.bfloat16), "img").astype(jnp.float32),
        lax.psum(up_weight_grad.astype(jnp.bfloat16), "img").astype(jnp.float32),
        lax.psum(up_bias_grad.astype(jnp.bfloat16), "img").astype(jnp.float32),
        lax.psum(down_weight_grad.astype(jnp.bfloat16), "img").astype(jnp.float32),
        lax.psum(down_bias_grad.astype(jnp.bfloat16), "img").astype(jnp.float32),
    )
    return (
        encoded,
        latent_grad[None],
        color_grad[None],
        replica_sums[0],
        replica_sums[1],
        replica_sums[2],
        replica_sums[3],
        pixel_sums[3],
        pixel_sums[4],
        pixel_sums[0],
        pixel_sums[1],
        pixel_sums[2],
        replica_sums[4],
        replica_sums[5],
        replica_sums[6],
        replica_sums[7],
        replica_sums[8],
        replica_sums[9],
    )


def solution(mesh):
    return jax.shard_map(
        shards,
        mesh=mesh,
        in_specs=(
            P("img", None, None),
            P("img", None, "pix"),
            P("img", None, "pix"),
            P("img", "pix"),
            P(),
            P(),
            P(),
            P(),
            P(),
            P(),
            P(),
            P(),
            P(),
            P(),
            P(),
            P(),
            P(),
            P(),
            P(),
            P("img", None, None),
        ),
        out_specs=(
            P("img", None, None),
            P("img", None, None),
            P("img", None, "pix"),
            P(),
            P(),
            P(),
            P(),
            P(),
            P(),
            P(),
            P(),
            P(),
            P(),
            P(),
            P(),
            P(),
            P(),
            P(),
        ),
        check_vma=False,
    )
```

profile of v0, /device:TPU:0, one launch (start us, length us, event | category | flops | bytes accessed | tf_op | source)
XLA Modules:
  0.0 493.2 jit_solution(3824822552677520739)
XLA Ops:
  7.3 0.8 fusion.175
  8.1 0.7 copy.47
  8.8 0.7 compare_reduce_fusion.1
  9.5 1.3 convert_reduce_fusion.2
  10.7 0.7 fusion.176
  12.2 1.6 fusion.121
  14.1 2.8 add_convert_fusion.1
  17.3 1.6 fusion.10
  20.1 3.0 select_reduce_fusion.1
  23.1 1.9 convolution_convert_fusion.3
  25.1 0.8 fusion.11
  26.7 43.5 %all-reduce.4 = (f32[256]{0:T(256)S(1)}, f32[256]{0:T(256)S(1)}) all-reduce(f32[256]{0:T(256)S(1)} %get-tuple-element.120, f32[256]{0:T(256)S(1)} %get-tuple-element.122), channel_id=1, replica_groups=mesh['img'=2,'pix'=16] {'pix'}, use_global_device_ids=true, to_apply=%region_5.6 | all-reduce | flops 512 | bytes 4096 | tf_op jit(solution)/shard_map/pmax | solution.py:75
  70.2 1.9 add_convert_fusion
  72.1 2.0 fusion.115
  74.1 2.0 fusion.118
  76.5 37.6 %psum.143 = f32[256]{0:T(256)S(1)} all-reduce(f32[256]{0:T(256)S(1)} %fusion.117), channel_id=1, replica_groups=mesh['img'=2,'pix'=16] {'pix'}, use_global_device_ids=true, to_apply=%region_19.20 | all-reduce | flops 256 | bytes 2048 | tf_op jit(solution)/shard_map/psum | solution.py:77
  114.0 1.8 fusion.114
  115.8 83.1 %all-reduce.14.cloned.1.call-done = (f32[256,1024]{1,0:T(8,128)}, f32[256,1024]{1,0:T(8,128)}) async-done(((f32[256,1024]{1,0:T(8,128)}, f32[256,1024]{1,0:T(8,128)}), (f32[256,1024]{1,0:T(8,128)}, f32[256,1024]{1,0:T(8,128)})) %all-reduce.14.cloned.1.call-update) | async-done | bytes 2097168 | tf_op jit(solution)/shard_map/psum | solution.py:77
  198.9 1.5 fusion.197
  200.8 0.8 convolution_add_fusion
  201.8 0.7 copy-done.75
  202.5 3.7 fusion.201
  206.3 1.6 multiply_reduce_fusion
  207.9 2.2 convolution_convert_fusion.1
  210.1 4.0 convolution_convert_fusion
  214.6 0.7 copy-done.4
  216.2 1.1 fusion.20
  217.4 1.4 convolution_multiply_fusion
  218.8 89.6 %all-reduce.17 = (f32[256]{0:T(256)}, bf16[256,1024]{1,0:T(8,128)(2,1)}) all-reduce(f32[256]{0:T(256)} %fusion.114, f32[256,1024]{1,0:T(8,128)} %convolution_multiply_fusion), channel_id=1, replica_groups=mesh['img'=2,'pix'=16] {'pix'}, use_global_device_ids=true, to_apply=%region_8.9 | all-reduce | flops 262400 | bytes 1574912 | tf_op jit(solution)/shard_map/psum | solution.py:77
  308.4 3.3 convolution_convert_fusion.2
  312.7 1.7 fusion.193
  314.4 1.0 copy-done.6
  315.8 2.2 fusion.191
  318.1 1.1 fusion.23
  320.7 1.0 convert_reduce_fusion
  323.2 1.5 fusion.186
  324.6 1.5 fusion.184
  326.2 3.0 add_bitcast_fusion
  329.3 0.9 copy-done.27
  330.9 3.3 all-reduce.5
  338.6 37.2 %all-reduce = (f32[261]{0:T(512)}, f32[261]{0:T(512)}, f32[1024]{0:T(1024)}) all-reduce(f32[261]{0:T(512)S(1)} %get-tuple-element.77, f32[261]{0:T(512)S(1)} %reduce_sum.377, f32[1024]{0:T(1024)S(1)} %get-tuple-element.129), channel_id=1, replica_groups=mesh['img'=2,'pix'=16] {'img','pix'}, use_global_device_ids=true, to_apply=%region_38.39 | all-reduce | flops 1546 | bytes 12368 | tf_op jit(solution)/shard_map/psum | solution.py:210
  375.8 6.7 %fusion.15 = bf16[1,256,1024]{2,1,0:T(8,128)(2,1)} fusion(f32[256,1024]{1,0:T(8,128)} %copy-done.6, bf16[1024,1024]{1,0:T(8,128)(2,1)} %param.37, bf16[1024,1024]{1,0:T(8,128)(2,1)S(1)} %copy-done, f32[1024]{0:T(1024)S(1)} %copy-done.82, f32[1024]{0:T(1024)S(1)} %copy-done.81, f32[1024]{0:T(1024)S(1)} %copy-done.60, f32[1024]{0:T(1024)S(1)} %copy-done.36, ...), kind=kOutput, calls=%fused_computation.39 | convolution fusion | flops 1093140480 | bytes 5785600 | tf_op jit(solution)/shard_map/dot_general | solution.py:85
  382.5 4.2 convert_element_type.211
  386.7 2.5 convert_element_type.219
  389.2 2.5 convert_element_type.223
  391.7 91.6 %all-reduce.12.cloned.1.call-done = (f32[261,1024]{1,0:T(8,128)}, f32[261,1024]{1,0:T(8,128)}) async-done(((f32[261,1024]{1,0:T(8,128)}, f32[261,1024]{1,0:T(8,128)}), (f32[261,1024]{1,0:T(8,128)}, f32[261,1024]{1,0:T(8,128)})) %all-reduce.12.cloned.1.call-update) | async-done | bytes 2138128 | tf_op jit(solution)/shard_map/psum | solution.py:210
  483.3 2.4 copy.59
  485.7 1.0 copy.60
  (220 shorter events, 14.8 us)
Async XLA Ops:
  7.2 193.5 %copy-start = (bf16[1024,1024]{1,0:T(8,128)(2,1)S(1)}, bf16[1024,1024]{1,0:T(8,128)(2,1)}, u32[]{:S(2)}) copy-start(bf16[1024,1024]{1,0:T(8,128)(2,1)} %param.35) | copy-start | bytes 6291460
  7.2 191.7 %all-reduce.14.cloned.1.call-start = ((), (), s32[]{:S(2)}) async-start(), calls=%async_computation.1 | async-start | bytes 4194304 | tf_op jit(solution)/shard_map/psum | solution.py:77
  9.5 7.5 %copy-start.1 = (bf16[1,256,1024]{2,1,0:T(8,128)(2,1)S(1)}, bf16[1,256,1024]{2,1,0:T(8,128)(2,1)}, u32[]{:S(2)}) copy-start(bf16[1,256,1024]{2,1,0:T(8,128)(2,1)} %param.20) | copy-start | bytes 1572868
  13.8 3.5 copy-start.32
  13.8 3.5 copy-start.72
  13.8 3.5 copy-start.77
  13.8 3.5 copy-start.79
  17.3 2.8 copy-start.28
  17.3 2.8 copy-start.51
  18.9 57.3 %copy-start.56 = (pred[384]{0:T(512)(128)(4,1)}, pred[384]{0:T(512)(128)(4,1)S(1)}, u32[]{:S(2)}) copy-start(pred[384]{0:T(512)(128)(4,1)S(1)} %compare_reduce_fusion) | copy-start | bytes 1156
  19.1 5.9 %copy-start.37 = (f32[256]{0:T(256)}, f32[256]{0:T(256)S(1)}, u32[]{:S(2)}) copy-start(f32[256]{0:T(256)S(1)} %broadcast_multiply_fusion.3) | copy-start | bytes 3076
  19.4 5.6 %copy-start.46 = (f32[256]{0:T(256)}, f32[256]{0:T(256)S(1)}, u32[]{:S(2)}) copy-start(f32[256]{0:T(256)S(1)} %fusion.137) | copy-start | bytes 3076
  20.1 4.9 %copy-start.30 = (f32[384]{0:T(512)}, f32[384]{0:T(512)S(1)}, u32[]{:S(2)}) copy-start(f32[384]{0:T(512)S(1)} %fusion.112) | copy-start | bytes 4612
  25.0 45.1 %copy-start.78 = (f32[1024]{0:T(1024)S(1)}, f32[1024]{0:T(1024)}, u32[]{:S(2)}) copy-start(f32[1024]{0:T(1024)} %param.32) | copy-start | bytes 12292
  26.7 49.5 %copy-start.11 = (f32[256,384]{1,0:T(8,128)}, f32[256,384]{1,0:T(8,128)S(1)}, u32[]{:S(2)}) copy-start(f32[256,384]{1,0:T(8,128)S(1)} %get-tuple-element.123) | copy-start | bytes 1179652
  70.2 6.0 %copy-start.61 = (f32[256]{0:T(256)}, f32[256]{0:T(256)S(1)}, u32[]{:S(2)}) copy-start(f32[256]{0:T(256)S(1)} %get-tuple-element.89) | copy-start | bytes 3076
  76.1 306.4 %all-reduce.16.cloned.1.call-start = ((), (), s32[]{:S(2)}) async-start(), calls=%async_computation.2 | async-start | bytes 12582912 | tf_op jit(solution)/shard_map/psum | solution.py:223
  76.4 124.3 %copy-start.35 = (f32[1024]{0:T(1024)S(1)}, f32[1024]{0:T(1024)}, u32[]{:S(2)}) copy-start(f32[1024]{0:T(1024)} %param.33) | copy-start | bytes 12292
  76.4 124.3 %copy-start.59 = (f32[1024]{0:T(1024)S(1)}, f32[1024]{0:T(1024)}, u32[]{:S(2)}) copy-start(f32[1024]{0:T(1024)} %param.34) | copy-start | bytes 12292
  76.5 124.3 %copy-start.80 = (f32[1024]{0:T(1024)S(1)}, f32[1024]{0:T(1024)}, u32[]{:S(2)}) copy-start(f32[1024]{0:T(1024)} %param.36) | copy-start | bytes 12292
  114.0 100.6 %copy-start.40 = (f32[256]{0:T(256)}, f32[256]{0:T(256)S(1)}, u32[]{:S(2)}) copy-start(f32[256]{0:T(256)S(1)} %psum.143) | copy-start | bytes 3076
  214.5 2.9 copy-start.2
  311.8 171.5 %all-reduce.12.cloned.1.call-start = ((), (), s32[]{:S(2)}) async-start(), calls=%async_computation | async-start | bytes 4325376 | tf_op jit(solution)/shard_map/psum | solution.py:210
  312.7 3.0 copy-start.26
  312.7 3.0 copy-start.74
  315.8 4.5 copy-start.23
  318.0 3.7 copy-start.5
  318.0 2.6 copy-start.13
  318.0 2.7 copy-start.25
  318.0 2.7 copy-start.41
  318.0 2.7 copy-start.58
  318.0 2.7 copy-start.63
  318.1 3.6 copy-start.44
  323.1 3.1 copy-start.34
  323.1 3.1 copy-start.39
  323.1 3.0 copy-start.43
  323.1 3.0 copy-start.45
  323.1 3.0 copy-start.48
  323.1 3.0 copy-start.64
  329.2 6.8 %copy-start.10 = (f32[384,261]{0,1:T(8,128)S(1)}, f32[384,261]{0,1:T(8,128)}, u32[]{:S(2)}) copy-start(f32[384,261]{0,1:T(8,128)} %copy-done.9) | copy-start | bytes 1202692
  329.2 46.6 %copy-start.36 = (f32[1024]{0:T(1024)S(1)}, f32[1024]{0:T(1024)}, u32[]{:S(2)}) copy-start(f32[1024]{0:T(1024)} %param.33) | copy-start | bytes 12292
  329.2 46.6 %copy-start.60 = (f32[1024]{0:T(1024)S(1)}, f32[1024]{0:T(1024)}, u32[]{:S(2)}) copy-start(f32[1024]{0:T(1024)} %param.34) | copy-start | bytes 12292
  329.2 46.5 %copy-start.66 = (f32[256]{0:T(256)S(1)}, f32[256]{0:T(256)}, u32[]{:S(2)}) copy-start(f32[256]{0:T(256)} %copy-done.65) | copy-start | bytes 3076
  329.2 46.5 %copy-start.71 = (f32[256]{0:T(256)S(1)}, f32[256]{0:T(256)}, u32[]{:S(2)}) copy-start(f32[256]{0:T(256)} %add_rsqrt_fusion.1) | copy-start | bytes 3076
  329.3 46.5 %copy-start.81 = (f32[1024]{0:T(1024)S(1)}, f32[1024]{0:T(1024)}, u32[]{:S(2)}) copy-start(f32[1024]{0:T(1024)} %param.36) | copy-start | bytes 12292
  329.3 46.5 %copy-start.82 = (f32[1024]{0:T(1024)S(1)}, f32[1024]{0:T(1024)}, u32[]{:S(2)}) copy-start(f32[1024]{0:T(1024)} %param.38) | copy-start | bytes 12292
  382.5 4.2 copy-start.8
  386.7 2.5 copy-start.7
  (38 other events, 60.4 us)
Sparse Core Ops, SparseCore 0:
  76.3 122.6 all-reduce.13
  311.9 28.9 all-reduce.15
  347.3 135.9 all-reduce.11
where the time goes:
time: 494 us; the launch traced here: 493 us
  blocking collectives  211 us (43%)
  waiting for transfers between devices  175 us (35%)
  matrix products  49 us (10%)
  other arithmetic  32.3 us (7%)
  between operations  14.9 us (3%)
  local copies, waits for them, and re-layouts  10.8 us (2%)
    psum x2, blocking collectives, forward_pass(): lax.psum((jnp.sum(weight, axis=1), jnp.dot(weight, values_full, precision...  127 us
    psum x1, waiting for transfers between devices, shards(): lax.psum((key_weight_grad, value_weight_grad, value_bias_grad, in_gain_co...  91.6 us
    psum x1, waiting for transfers between devices, forward_pass(): lax.psum((jnp.sum(weight, axis=1), jnp.dot(weight, values_full, precision...  83.1 us
    pmax x1, blocking collectives, forward_pass(): row_top = lax.pmax(local_top, 'pix')  43.5 us
    psum x1, blocking collectives, shards(): lax.psum((key_weight_grad, value_weight_grad, value_bias_grad, in_gain_co...  37.2 us
    dot_general x18, matrix products, contract(): lax.dot_general(left, right, (((left_dim,), (right_dim,)), ((), ())), pre...  33.8 us
    unnamed x170, local copies, waits for them, and re-layouts  10.1 us
  transfers between devices with their start and end apart: 3, of which 2 were waited for; matrix products, arithmetic and copies ran while one was open for 8% of the time, Pallas kernels for 0%

commit v1 on v0

--- a/solution.py
+++ b/solution.py
@@ -207,16 +207,14 @@
     ignored, latent_pull = jax.vjp(partial(norm_axis, axis_pos=1), latent, lat_gain, lat_shift)
     latent_part, lat_gain_grad, lat_shift_grad = latent_pull(norm_one_grad)
     latent_grad = mixed_grad + latent_part
-    pixel_sums = lax.psum(
-        (
-            key_weight_grad,
-            value_weight_grad,
-            value_bias_grad,
-            in_gain_col[:, 0],
-            in_shift_col[:, 0],
-        ),
-        ("img", "pix"),
-    )
+    array_here = (
+        key_weight_grad,
+        value_weight_grad,
+        value_bias_grad,
+        in_gain_col[:, 0],
+        in_shift_col[:, 0],
+    )
+    pixel_sums = lax.psum(lax.psum(array_here, "pix"), "img")
     replica_sums = (
         lax.psum(lat_gain_grad.astype(jnp.bfloat16), "img").astype(jnp.float32),
         lax.psum(lat_shift_grad.astype(jnp.bfloat16), "img").astype(jnp.float32),

time: 494 us -> 430 us (0.87)
  waiting for transfers between devices: 175 us -> 132 us
  blocking collectives: 211 us -> 185 us
    psum x1, waiting for transfers between devices: 91.6 us -> 15.8 us  [shards(): pixel_sums = lax.psum(lax.psum(array_here, 'pix'), 'img')]
    psum x1, blocking collectives: 37.2 us -> 3.06 us  [shards(): pixel_sums = lax.psum(lax.psum(array_here, 'pix'), 'img')]
    psum x1, waiting for transfers between devices: 0.01 us -> 24.5 us  [shards(): lax.psum(query_weight_grad.astype(jnp.bfloat16), 'img').astype(jnp.float32)]
    psum x1 -> x2, waiting for transfers between devices: 83.1 us -> 92 us  [forward_pass(): lax.psum((jnp.sum(weight, axis=1), jnp.dot(weight, values_full, precision...]
    psum x2, blocking collectives: 127 us -> 136 us  [forward_pass(): lax.psum((jnp.sum(weight, axis=1), jnp.dot(weight, values_full, precision...]
    unnamed x170 -> x132, local copies, waits for them, and re-layouts: 10.1 us -> 11.9 us
  transfers between devices with their start and end apart: 3 -> 4, of which waited for: 2 -> 4; matrix products, arithmetic and copies ran while one was open for 8% -> 12% of each run, Pallas kernels for 0% -> 0%
where the time goes in v1:
time: 430 us; the launch traced here: 429 us
  blocking collectives  185 us (43%)
  waiting for transfers between devices  132 us (31%)
  matrix products  51 us (12%)
  other arithmetic  33 us (8%)
  between operations  14.6 us (3%)
  local copies, waits for them, and re-layouts  12.7 us (3%)
    psum x2, blocking collectives, forward_pass(): lax.psum((jnp.sum(weight, axis=1), jnp.dot(weight, values_full, precision...  136 us
    psum x2, waiting for transfers between devices, forward_pass(): lax.psum((jnp.sum(weight, axis=1), jnp.dot(weight, values_full, precision...  92 us
    pmax x1, blocking collectives, forward_pass(): row_top = lax.pmax(local_top, 'pix')  43.5 us
    dot_general x18, matrix products, contract(): lax.dot_general(left, right, (((left_dim,), (right_dim,)), ((), ())), pre...  33.1 us
    psum x1, waiting for transfers between devices, shards(): lax.psum(query_weight_grad.astype(jnp.bfloat16), 'img').astype(jnp.float32)  24.5 us
    psum x1, waiting for transfers between devices, shards(): pixel_sums = lax.psum(lax.psum(array_here, 'pix'), 'img')  15.8 us
    unnamed x132, local copies, waits for them, and re-layouts  11.9 us
  transfers between devices with their start and end apart: 4, of which 4 were waited for; matrix products, arithmetic and copies ran while one was open for 12% of the time, Pallas kernels for 0%

profile of v1, /device:TPU:0, one launch (start us, length us, event | category | flops | bytes accessed | tf_op | source)
XLA Modules:
  0.0 429.3 jit_solution(7070723672133240074)
XLA Ops:
  7.3 0.8 fusion.175
  9.6 1.2 convert_reduce_fusion.2
  12.2 1.6 fusion.121
  14.1 1.3 fusion.24
  15.5 3.2 fusion.10
  19.8 2.3 select_reduce_fusion.1
  22.1 2.0 convolution_convert_fusion.3
  24.1 0.8 fusion.11
  25.0 1.2 select_reduce_fusion
  26.3 43.5 %all-reduce.2 = (f32[256]{0:T(256)S(1)}, f32[256]{0:T(256)S(1)}) all-reduce(f32[256]{0:T(256)S(1)} %get-tuple-element.124, f32[256]{0:T(256)S(1)} %get-tuple-element.126), channel_id=1, replica_groups=mesh['img'=2,'pix'=16] {'pix'}, use_global_device_ids=true, to_apply=%region_5.6 | all-reduce | flops 512 | bytes 4096 | tf_op jit(solution)/shard_map/pmax | solution.py:75
  69.7 1.8 add_convert_fusion
  71.6 0.9 copy-done.22
  72.5 2.0 fusion.118
  74.5 1.2 fusion.117
  75.8 37.0 %psum.178 = f32[256]{0:T(256)S(1)} all-reduce(f32[256]{0:T(256)S(1)} %fusion.117), channel_id=1, replica_groups=mesh['img'=2,'pix'=16] {'pix'}, use_global_device_ids=true, to_apply=%region_19.20 | all-reduce | flops 256 | bytes 2048 | tf_op jit(solution)/shard_map/psum | solution.py:77
  112.8 1.8 add_convert_fusion.1
  114.6 2.0 fusion.115
  116.6 65.7 %all-reduce.13.cloned.1.call-done = f32[256,1024]{1,0:T(8,128)} async-done(((f32[256,1024]{1,0:T(8,128)}), f32[256,1024]{1,0:T(8,128)}) %all-reduce.13.cloned.1.call-update) | async-done | bytes 1048592 | tf_op jit(solution)/shard_map/psum | solution.py:77
  182.3 1.5 fusion.197
  184.2 0.8 convolution_add_fusion
  186.0 3.7 fusion.201
  189.7 1.6 multiply_reduce_fusion
  193.1 1.5 convert_reduce_fusion
  196.4 1.5 fusion.186
  197.8 1.5 fusion.184
  199.4 1.9 fusion.114
  201.4 2.7 convolution_multiply_fusion
  205.4 98.6 %all-reduce.20 = (f32[256]{0:T(256)S(1)}, bf16[256,1024]{1,0:T(8,128)(2,1)}, f32[261]{0:T(512)S(1)}, f32[261]{0:T(512)S(1)}, f32[1024]{0:T(1024)S(1)}) all-reduce(f32[256]{0:T(256)S(1)} %copy-done.48, f32[256,1024]{1,0:T(8,128)} %convolution_multiply_fusion, f32[261]{0:T(512)S(1)} %get-tuple-element.77, ...), channel_id=1, replica_groups=mesh['img'=2,'pix'=16] {'pix'}, use_global_device_ids=true, to_apply=%region_8.9 | all-reduce | flops 263946 | bytes 1587280 | tf_op jit(solution)/shard_map/psum | solution.py:77
  304.0 3.4 convolution_convert_fusion.2
  307.4 2.2 convolution_convert_fusion.1
  309.6 4.0 convolution_convert_fusion
  314.5 1.2 fusion.192
  316.3 1.1 convert_reduce_fusion.5
  317.5 2.7 fusion.191
  320.2 1.0 copy-done.7
  321.8 3.3 all-reduce.5
  329.3 3.1 all-reduce.3
  332.3 26.3 %all-reduce.15.cloned.1.call-done = (f32[256,1024]{1,0:T(8,128)}, f32[261,1024]{1,0:T(8,128)}, f32[261,1024]{1,0:T(8,128)}) async-done(((f32[256,1024]{1,0:T(8,128)}, f32[261,1024]{1,0:T(8,128)}, f32[261,1024]{1,0:T(8,128)}), (f32[256,1024]{1,0:T(8,128)}, f32[261,1024]{1,0:T(8,128)}, f32[261,1024]{1,0:T(8,128)})) %all-reduce.15.cloned.1.call-update) | async-done | bytes 3186704 | tf_op jit(solution)/shard_map/psum | solution.py:77
  358.7 3.1 add_bitcast_fusion
  362.1 1.0 copy-done.9
  363.3 6.5 %fusion.15 = bf16[1,256,1024]{2,1,0:T(8,128)(2,1)} fusion(f32[256,1024]{1,0:T(8,128)} %copy-done.9, bf16[1024,1024]{1,0:T(8,128)(2,1)} %param.37, bf16[1024,1024]{1,0:T(8,128)(2,1)S(1)} %copy-done, f32[1024]{0:T(1024)S(1)} %copy-done.61, f32[1024]{0:T(1024)S(1)} %copy-done.60, f32[1024]{0:T(1024)S(1)} %copy-done.45, f32[1024]{0:T(1024)S(1)} %copy-done.35, ...), kind=kOutput, calls=%fused_computation.39 | convolution fusion | flops 1093140480 | bytes 5785600 | tf_op jit(solution)/shard_map/dot_general | solution.py:85
  369.9 24.5 %all-reduce.19.cloned.1.call-done = (bf16[1024,1024]{1,0:T(8,128)(2,1)}, bf16[1024,1024]{1,0:T(8,128)(2,1)}, bf16[1024,1024]{1,0:T(8,128)(2,1)}) async-done(((bf16[1024,1024]{1,0:T(8,128)(2,1)}, bf16[1024,1024]{1,0:T(8,128)(2,1)}, bf16[1024,1024]{1,0:T(8,128)(2,1)}), (bf16[1024,1024]{1,0:T(8,128)(2,1)}, bf16[1024,1024]{1,0:T(8,128)(2,1)}, bf16[1024,1024]{1,0:T(8,128)(2,1)})) %all-reduce.19.cloned.1.call-update) | async-done | bytes 6291472 | tf_op jit(solution)/shard_map/psum | solution.py:221
  394.4 4.2 convert_element_type.211
  398.6 2.5 convert_element_type.219
  401.1 2.5 convert_element_type.223
  403.6 15.8 %all-reduce.17.cloned.1.call-done = (f32[261,1024]{1,0:T(8,128)}, f32[261,1024]{1,0:T(8,128)}) async-done(((f32[261,1024]{1,0:T(8,128)}, f32[261,1024]{1,0:T(8,128)}), (f32[261,1024]{1,0:T(8,128)}, f32[261,1024]{1,0:T(8,128)})) %all-reduce.17.cloned.1.call-update) | async-done | bytes 2138128 | tf_op jit(solution)/shard_map/psum | solution.py:217
  419.3 2.4 copy.64
  421.8 1.0 copy.65
  (185 shorter events, 17.5 us)
Async XLA Ops:
  7.2 176.9 %copy-start = (bf16[1024,1024]{1,0:T(8,128)(2,1)S(1)}, bf16[1024,1024]{1,0:T(8,128)(2,1)}, u32[]{:S(2)}) copy-start(bf16[1024,1024]{1,0:T(8,128)(2,1)} %param.35) | copy-start | bytes 6291460
  7.2 8.2 %copy-start.1 = (bf16[1,256,1024]{2,1,0:T(8,128)(2,1)S(1)}, bf16[1,256,1024]{2,1,0:T(8,128)(2,1)}, u32[]{:S(2)}) copy-start(bf16[1,256,1024]{2,1,0:T(8,128)(2,1)} %param.20) | copy-start | bytes 1572868
  7.2 8.2 %copy-start.34 = (f32[1024]{0:T(1024)S(1)}, f32[1024]{0:T(1024)}, u32[]{:S(2)}) copy-start(f32[1024]{0:T(1024)} %param.24) | copy-start | bytes 12292
  7.2 8.2 %copy-start.57 = (f32[1024]{0:T(1024)S(1)}, f32[1024]{0:T(1024)}, u32[]{:S(2)}) copy-start(f32[1024]{0:T(1024)} %param.25) | copy-start | bytes 12292
  7.2 8.2 %copy-start.55 = (f32[1024]{0:T(1024)S(1)}, f32[1024]{0:T(1024)}, u32[]{:S(2)}) copy-start(f32[1024]{0:T(1024)} %param.27) | copy-start | bytes 12292
  7.2 175.1 %all-reduce.13.cloned.1.call-start = ((), (), s32[]{:S(2)}) async-start(), calls=%async_computation | async-start | bytes 2097152 | tf_op jit(solution)/shard_map/psum | solution.py:77
  9.5 105.0 %copy-start.43 = (pred[384]{0:T(512)(128)(4,1)}, pred[384]{0:T(512)(128)(4,1)S(1)}, u32[]{:S(2)}) copy-start(pred[384]{0:T(512)(128)(4,1)S(1)} %compare_reduce_fusion.1) | copy-start | bytes 1156
  13.8 55.9 %copy-start.10 = (bf16[128,384]{1,0:T(8,128)(2,1)}, bf16[128,384]{1,0:T(8,128)(2,1)S(1)}, u32[]{:S(2)}) copy-start(bf16[128,384]{1,0:T(8,128)(2,1)S(1)} %get-tuple-element.115) | copy-start | bytes 294916
  15.5 3.2 copy-start.42
  15.5 4.3 %copy-start.33 = (f32[261]{0:T(512)S(1)}, f32[261]{0:T(512)}, u32[]{:S(2)}) copy-start(f32[261]{0:T(512)} %param.28) | copy-start | bytes 3136
  15.5 4.3 %copy-start.40 = (f32[261]{0:T(512)S(1)}, f32[261]{0:T(512)}, u32[]{:S(2)}) copy-start(f32[261]{0:T(512)} %param.29) | copy-start | bytes 3136
  22.1 92.4 %copy-start.17 = (f32[256,384]{1,0:T(8,128)}, f32[256,384]{1,0:T(8,128)S(1)}, u32[]{:S(2)}) copy-start(f32[256,384]{1,0:T(8,128)S(1)} %get-tuple-element.125) | copy-start | bytes 1179652
  22.1 2.0 copy-start.52
  24.1 45.6 %copy-start.56 = (f32[1024]{0:T(1024)S(1)}, f32[1024]{0:T(1024)}, u32[]{:S(2)}) copy-start(f32[1024]{0:T(1024)} %param.32) | copy-start | bytes 12292
  69.7 44.8 %copy-start.47 = (f32[256]{0:T(256)}, f32[256]{0:T(256)S(1)}, u32[]{:S(2)}) copy-start(f32[256]{0:T(256)S(1)} %get-tuple-element.87) | copy-start | bytes 3076
  69.7 2.7 copy-start.18
  74.5 284.1 %all-reduce.15.cloned.1.call-start = ((), (), s32[]{:S(2)}) async-start(), calls=%async_computation.1 | async-start | bytes 6422528 | tf_op jit(solution)/shard_map/psum | solution.py:77
  116.6 67.5 %copy-start.35 = (f32[1024]{0:T(1024)S(1)}, f32[1024]{0:T(1024)}, u32[]{:S(2)}) copy-start(f32[1024]{0:T(1024)} %param.33) | copy-start | bytes 12292
  116.6 67.5 %copy-start.44 = (f32[1024]{0:T(1024)S(1)}, f32[1024]{0:T(1024)}, u32[]{:S(2)}) copy-start(f32[1024]{0:T(1024)} %param.34) | copy-start | bytes 12292
  116.6 67.5 %copy-start.59 = (f32[1024]{0:T(1024)S(1)}, f32[1024]{0:T(1024)}, u32[]{:S(2)}) copy-start(f32[1024]{0:T(1024)} %param.36) | copy-start | bytes 12292
  183.8 7.5 %copy-start.2 = (f32[256,1024]{1,0:T(8,128)}, f32[256,1024]{1,0:T(8,128)S(1)}, u32[]{:S(2)}) copy-start(f32[256,1024]{1,0:T(8,128)S(1)} %get-tuple-element.113) | copy-start | bytes 3145732
  184.1 7.2 %copy-start.36 = (f32[256]{0:T(256)}, f32[256]{0:T(256)S(1)}, u32[]{:S(2)}) copy-start(f32[256]{0:T(256)S(1)} %fusion.138) | copy-start | bytes 3076
  184.2 1.8 copy-start.53
  186.0 3.8 copy-start.62
  191.7 2.9 copy-start.4
  194.6 3.2 copy-start.24
  199.3 195.0 %all-reduce.19.cloned.1.call-start = ((), (), s32[]{:S(2)}) async-start(), calls=%async_computation.3 | async-start | bytes 12582912 | tf_op jit(solution)/shard_map/psum | solution.py:221
  199.4 4.6 %copy-start.28 = (bf16[261,1024]{1,0:T(8,128)(2,1)S(1)}, bf16[261,1024]{1,0:T(8,128)(2,1)}, u32[]{:S(2)}) copy-start(bf16[261,1024]{1,0:T(8,128)(2,1)} %param.30) | copy-start | bytes 1603588
  199.4 5.1 %copy-start.12 = (bf16[128,384]{1,0:T(8,128)(2,1)S(1)}, bf16[128,384]{1,0:T(8,128)(2,1)}, u32[]{:S(2)}) copy-start(bf16[128,384]{1,0:T(8,128)(2,1)} %copy-done.10) | copy-start | bytes 294916
  199.4 5.1 %copy-start.25 = (bf16[384,1024]{1,0:T(8,128)(2,1)S(1)}, bf16[384,1024]{1,0:T(8,128)(2,1)}, u32[]{:S(2)}) copy-start(bf16[384,1024]{1,0:T(8,128)(2,1)} %copy-done.24) | copy-start | bytes 2359300
  199.4 5.1 %copy-start.54 = (bf16[261,1024]{1,0:T(8,128)(2,1)S(1)}, bf16[261,1024]{1,0:T(8,128)(2,1)}, u32[]{:S(2)}) copy-start(bf16[261,1024]{1,0:T(8,128)(2,1)} %param.31) | copy-start | bytes 1603588
  204.5 99.4 %copy-start.58 = (f32[1024]{0:T(1024)S(1)}, f32[1024]{0:T(1024)}, u32[]{:S(2)}) copy-start(f32[1024]{0:T(1024)} %param.25) | copy-start | bytes 12292
  205.2 98.8 %copy-start.16 = (f32[384,261]{0,1:T(8,128)}, f32[384,261]{0,1:T(8,128)S(1)}, u32[]{:S(2)}) copy-start(f32[384,261]{0,1:T(8,128)S(1)} %get-tuple-element.129) | copy-start | bytes 1202692
  205.3 102.0 %copy-start.37 = (f32[256]{0:T(256)S(1)}, f32[256]{0:T(256)}, u32[]{:S(2)}) copy-start(f32[256]{0:T(256)} %copy-done.36) | copy-start | bytes 3076
  205.4 102.0 %copy-start.45 = (f32[1024]{0:T(1024)S(1)}, f32[1024]{0:T(1024)}, u32[]{:S(2)}) copy-start(f32[1024]{0:T(1024)} %param.34) | copy-start | bytes 12292
  304.0 3.4 copy-start.3
  304.0 3.4 copy-start.30
  307.4 2.3 copy-start.6
  307.4 2.2 copy-start.63
  313.7 105.7 %all-reduce.17.cloned.1.call-start = ((), (), s32[]{:S(2)}) async-start(), calls=%async_computation.2 | async-start | bytes 4325376 | tf_op jit(solution)/shard_map/psum | solution.py:217
  317.5 2.7 copy-start.39
  317.5 4.3 %copy-start.49 = (bf16[1024]{0:T(1024)(128)(2,1)S(1)}, bf16[1024]{0:T(1024)(128)(2,1)}, u32[]{:S(2)}) copy-start(bf16[1024]{0:T(1024)(128)(2,1)} %get-tuple-element.133) | copy-start | bytes 6148
  317.5 4.3 %copy-start.50 = (bf16[1024]{0:T(1024)(128)(2,1)S(1)}, bf16[1024]{0:T(1024)(128)(2,1)}, u32[]{:S(2)}) copy-start(bf16[1024]{0:T(1024)(128)(2,1)} %get-tuple-element.70) | copy-start | bytes 6148
  317.5 4.3 %copy-start.51 = (bf16[1024]{0:T(1024)(128)(2,1)S(1)}, bf16[1024]{0:T(1024)(128)(2,1)}, u32[]{:S(2)}) copy-start(bf16[1024]{0:T(1024)(128)(2,1)} %get-tuple-element.74) | copy-start | bytes 6148
  358.7 3.1 copy-start.21
  394.4 4.2 copy-start.15
  398.6 2.5 copy-start.14
  419.3 2.4 copy-start.20
  (20 other events, 23.6 us)
Sparse Core Ops, SparseCore 0:
  74.6 107.6 all-reduce.12
  199.5 159.1 all-reduce.14
  363.1 31.2 all-reduce.18
  396.7 22.5 all-reduce.16
